TPU v7x, 32 devices: a whole 2x2x4 slice. The times are simulated.
32 devices in a mesh: dp: 8 (over z, y), ctx: 4 (over x, core).
Axes of the slice: x: 2, y: 2, z: 4, core: 2. Of those that a mesh axis runs over, the one named last changes fastest.
Arguments:
- projected: bfloat16 [8, 512, 3, 4096], P('dp', 'ctx'), may hold values from -6 to 6
- short_taps: float32 [3, 3, 4096], P(None, None, 'ctx'), may hold values from -3 to 3
- long_filter: bfloat16 [512, 4096], P('dp', 'ctx'), may hold values from -1.1 to 1.1
- skip_gain: float32 [4096], P('ctx'), may hold values from -4 to 4
Outputs:
- mixed: bfloat16 [8, 512, 4096], P('dp', 'ctx')
All inputs are finite; a program needn't handle non-finite values.
Results may differ from a plain program's by a relative error of at most 0.012.
Values may be sent and summed in bfloat16 or wider, within the bound.
A program may use at most 64 MiB of HBM per device.

v0:
```python
import math
import jax
import jax.numpy as jnp
import numpy as np
from jax import lax
from jax.sharding import PartitionSpec as P

RADIX = 64
HIGH = lax.Precision.HIGHEST


def causal_short(extended, taps, kernel_size):
    row_count = extended.shape[0] - (kernel_size - 1)
    widened = extended.astype(jnp.float32)
    summed = jnp.zeros((row_count,) + widened.shape[1:], jnp.float32)
    for tap_index in range(kernel_size):
        offset = kernel_size - 1 - tap_index
        summed = summed + taps[tap_index] * widened[offset : offset + row_count]
    return (summed[:, 0].astype(jnp.bfloat16), (summed[:, 1] * summed[:, 2]).astype(jnp.bfloat16))


def dft_tables(length, radix_size):
    outer_size = 2 * length // radix_size
    total_size = outer_size * radix_size
    outer_range = jnp.arange(outer_size, dtype=jnp.int32)
    inner_range = jnp.arange(radix_size, dtype=jnp.int32)
    angle_one = (
        2.0
        * math.pi
        / outer_size
        * (outer_range[:, None] * outer_range[None, :] % outer_size).astype(jnp.float32)
    )
    angle_twist = (
        2.0
        * math.pi
        / total_size
        * (outer_range[:, None] * inner_range[None, :] % total_size).astype(jnp.float32)
    )
    angle_two = (
        2.0
        * math.pi
        / radix_size
        * (inner_range[:, None] * inner_range[None, :] % radix_size).astype(jnp.float32)
    )
    twist_cos = jnp.cos(angle_twist)[:, :, None]
    twist_sin = jnp.sin(angle_twist)[:, :, None]
    return (
        jnp.cos(angle_one),
        jnp.sin(angle_one),
        twist_cos,
        twist_sin,
        jnp.cos(angle_two),
        jnp.sin(angle_two),
    )


def forward_dft(signal, tables, radix_size):
    cos_one, sin_one, twist_cos, twist_sin, cos_two, sin_two = tables
    outer_size = cos_one.shape[0]
    half_size = outer_size // 2
    block_width = signal.shape[1]
    shaped = signal.reshape(half_size, radix_size * block_width)
    first_re = jnp.dot(cos_one[:, :half_size], shaped, precision=HIGH).reshape(
        outer_size, radix_size, block_width
    )
    first_im = -jnp.dot(sin_one[:, :half_size], shaped, precision=HIGH).reshape(
        outer_size, radix_size, block_width
    )
    second_re = first_re * twist_cos + first_im * twist_sin
    second_im = first_im * twist_cos - first_re * twist_sin
    spec_re = jnp.einsum("amc,mb->abc", second_re, cos_two, precision=HIGH) + jnp.einsum(
        "amc,mb->abc", second_im, sin_two, precision=HIGH
    )
    spec_im = jnp.einsum("amc,mb->abc", second_im, cos_two, precision=HIGH) - jnp.einsum(
        "amc,mb->abc", second_re, sin_two, precision=HIGH
    )
    return (spec_re, spec_im)


def inverse_dft(spec_re, spec_im, tables, radix_size):
    cos_one, sin_one, twist_cos, twist_sin, cos_two, sin_two = tables
    outer_size = cos_one.shape[0]
    half_size = outer_size // 2
    block_width = spec_re.shape[2]
    back_re = jnp.einsum("abc,mb->amc", spec_re, cos_two, precision=HIGH) - jnp.einsum(
        "abc,mb->amc", spec_im, sin_two, precision=HIGH
    )
    back_im = jnp.einsum("abc,mb->amc", spec_re, sin_two, precision=HIGH) + jnp.einsum(
        "abc,mb->amc", spec_im, cos_two, precision=HIGH
    )
    turned_re = (back_re * twist_cos - back_im * twist_sin).reshape(
        outer_size, radix_size * block_width
    )
    turned_im = (back_re * twist_sin + back_im * twist_cos).reshape(
        outer_size, radix_size * block_width
    )
    result = jnp.dot(cos_one[:half_size], turned_re, precision=HIGH) - jnp.dot(
        sin_one[:half_size], turned_im, precision=HIGH
    )
    return result.reshape(half_size * radix_size, block_width) / (outer_size * radix_size)


def long_convolve_blocked(gated_slab, filter_slab):
    length, channels = gated_slab.shape
    block_width = min(128, channels)
    tables = dft_tables(length, RADIX)

    def one_block(block_index, output):
        offset = block_index * block_width
        signal = lax.dynamic_slice_in_dim(gated_slab, offset, block_width, 1).astype(jnp.float32)
        kernel_block = lax.dynamic_slice_in_dim(filter_slab, offset, block_width, 1).astype(
            jnp.float32
        )
        sig_re, sig_im = forward_dft(signal, tables, RADIX)
        ker_re, ker_im = forward_dft(kernel_block, tables, RADIX)
        prod_re = sig_re * ker_re - sig_im * ker_im
        prod_im = sig_re * ker_im + sig_im * ker_re
        result = inverse_dft(prod_re, prod_im, tables, RADIX)
        return lax.dynamic_update_slice_in_dim(output, result, offset, 1)

    return lax.fori_loop(
        0, channels // block_width, one_block, jnp.zeros((length, channels), jnp.float32)
    )


def long_convolve(gated_slab, filter_slab):
    length = gated_slab.shape[0]
    if length > 1024:
        return long_convolve_blocked(gated_slab, filter_slab)
    forward, backward = quarter_tables(length)
    sig = jnp.dot(forward, gated_slab, preferred_element_type=jnp.float32)
    ker = jnp.dot(forward, filter_slab, preferred_element_type=jnp.float32)
    sig_cos, sig_sin, ker_cos, ker_sin = (sig[:length], sig[length:], ker[:length], ker[length:])
    prod = jnp.concatenate(
        [sig_cos * ker_cos - sig_sin * ker_sin, sig_cos * ker_sin + sig_sin * ker_cos]
    ).astype(jnp.bfloat16)
    return jnp.dot(backward, prod, preferred_element_type=jnp.float32)


def quarter_tables(length):
    steps = (4 * np.arange(length)[:, None] + 1) * np.arange(length)[None, :] % (4 * length)
    angles = steps * (2.0 * math.pi / (4 * length))
    table = np.concatenate([np.cos(angles), np.sin(angles)])
    return (jnp.asarray(table, jnp.bfloat16), jnp.asarray(table.T / length, jnp.bfloat16))


def make_response(gated_slab, filter_slab, skip_gain):
    long_part = long_convolve(gated_slab, filter_slab)
    return (long_part + skip_gain * gated_slab.astype(jnp.float32)).astype(jnp.bfloat16)


def combine_rows(query_part, response_part):
    return (query_part.astype(jnp.float32) * response_part.astype(jnp.float32)).astype(jnp.bfloat16)


def on_device(projected, short_taps, long_filter, skip_gain):
    kernel_size = short_taps.shape[0]
    ctx_size = lax.axis_size("ctx")
    rows = projected[0]
    filter_slab = lax.all_gather(long_filter, "dp", axis=0, tiled=True)
    all_taps = lax.all_gather(short_taps, "ctx", axis=2, tiled=True)
    halo = lax.ppermute(
        rows[-(kernel_size - 1) :], "ctx", [(i, i + 1) for i in range(ctx_size - 1)]
    )
    queries, gated = causal_short(jnp.concatenate([halo, rows]), all_taps, kernel_size)
    gated_slab = lax.all_to_all(gated, "ctx", split_axis=1, concat_axis=0, tiled=True)
    response_slab = make_response(gated_slab, filter_slab, skip_gain)
    response = lax.all_to_all(response_slab, "ctx", split_axis=0, concat_axis=1, tiled=True)
    return combine_rows(queries, response)[None]


def solution(mesh):
    return jax.shard_map(
        on_device,
        mesh=mesh,
        in_specs=(P("dp", "ctx", None, None), P(None, None, "ctx"), P("dp", "ctx"), P("ctx")),
        out_specs=P("dp", "ctx", None),
        check_vma=False,
    )
```

profile of v0, /device:TPU:0, one launch (start us, length us, event | category | flops | bytes accessed | tf_op | source)
XLA Modules:
  0.0 98.3 jit_solution(9374394444664084530)
XLA Ops:
  6.5 0.0 all-gather.2.cloned.1.call-start
  6.5 1.0 slice_bitcast_fusion.3
  7.5 2.4 %collective-permute-start = (bf16[2,3,4096]{2,0,1:T(2,128)(2,1)S(1)}, bf16[2,3,4096]{2,0,1:T(2,128)(2,1)S(1)}, u32[]{:S(2)}, u32[]{:S(2)}) collective-permute-start(bf16[2,3,4096]{2,0,1:T(2,128)(2,1)S(1)} %slice_bitcast_fusion.3), channel_id=1, source_target_pairs={{0,1},{1,2},{2,3},{4,5},{5,6},{6,7},{8,9},{9,10},{10,11},{12,13},{... | collective-permute-start | bytes 147464 | tf_op jit(solution)/shard_map/ppermute | solution.py:162
  9.9 0.0 all-gather.2.cloned.1.call-update
  9.9 7.1 %all_gather.6 = f32[3,3,4096]{2,1,0:T(4,128)S(1)} all-gather(f32[3,3,1024]{2,1,0:T(4,128)} %param.7), channel_id=1, replica_groups=mesh['dp'=8,'ctx'=4] {'ctx'}, dimensions={2}, use_global_device_ids=true | all-gather | bytes 184320 | tf_op jit(solution)/shard_map/all_gather | solution.py:161
  17.1 3.5 %copy.19 = bf16[1,128,3,4096]{1,3,2,0:T(8,128)(2,1)S(1)} copy(bf16[1,128,3,4096]{3,1,2,0:T(8,128)(2,1)} %param.6) | data formatting | bytes 6291456 | tf_op args[0]
  20.6 0.0 collective-permute-done
  20.6 2.8 %copy.20 = bf16[2,3,4096]{0,2,1:T(8,128)(2,1)} copy(bf16[2,3,4096]{2,0,1:T(2,128)(2,1)S(1)} %collective-permute-done) | data formatting | bytes 98304 | tf_op jit(solution)/shard_map/ppermute | solution.py:162
  23.4 4.1 %maximum_convert_fusion = f32[130,3,4096]{0,2,1:T(8,128)S(1)} fusion(bf16[128,3,4096]{0,2,1:T(8,128)(2,1)S(1)} %bitcast.36, bf16[2,3,4096]{0,2,1:T(8,128)(2,1)} %copy.20), kind=kLoop, calls=%fused_computation.5 | loop fusion | flops 6389760 | bytes 9584640 | tf_op jit(solution)/shard_map/convert_element_type | solution.py:14
  27.5 9.4 %fusion = f32[128,3,4096]{0,2,1:T(8,128)S(1)} fusion(f32[130,3,4096]{0,2,1:T(8,128)S(1)} %maximum_convert_fusion, f32[3,4096]{1,0:T(4,128)S(1)} %get-tuple-element.6, f32[3,4096]{1,0:T(4,128)S(1)} %get-tuple-element.7, f32[3,4096]{1,0:T(4,128)S(1)} %get-tuple-element.5), kind=kLoop, calls=%fused_computation.1 | loop fusion | flops 7864320 | bytes 25313280 | tf_op jit(solution)/shard_map/add | solution.py:18
  36.9 0.0 copy-start
  36.9 2.7 %copy-done = f32[128,3,4096]{0,2,1:T(8,128)} copy-done((f32[128,3,4096]{0,2,1:T(8,128)}, f32[128,3,4096]{0,2,1:T(8,128)S(1)}, u32[]{:S(2)}) %copy-start) | copy-done | bytes 6291480
  39.5 0.2 fusion.2
  39.7 0.5 copy.21
  40.3 16.9 %all_to_all.29 = bf16[128,4,1024]{2,0,1:T(8,128)(2,1)S(1)} all-to-all(bf16[128,4,1024]{2,0,1:T(8,128)(2,1)S(1)} %copy.21), channel_id=1, replica_groups=mesh['dp'=8,'ctx'=4] {'ctx'}, dimensions={1} | all-to-all | bytes 2097152 | tf_op jit(solution)/shard_map/all_to_all | solution.py:166
  57.2 0.8 copy.22
  58.0 0.3 reshape.46
  58.3 4.5 %fusion.8 = f32[1024,1024]{1,0:T(8,128)} fusion(bf16[1024,512]{1,0:T(8,128)(2,1)} %constant.9, bf16[512,1024]{1,0:T(8,128)(2,1)S(1)} %reshape.46), kind=kOutput, calls=%fused_computation.23 | convolution fusion | flops 1073741824 | bytes 6291456 | tf_op jit(solution)/shard_map/dot_general | solution.py:131
  62.8 0.0 copy-start.3
  62.8 0.0 all-gather.2.cloned.1.call-done
  62.8 0.0 copy-start.1
  62.8 2.9 %fusion.9 = f32[1024,1024]{1,0:T(8,128)S(1)} fusion(bf16[1024,512]{1,0:T(8,128)(2,1)} %constant.4.clone, bf16[512,1024]{1,0:T(8,128)(2,1)} %all-gather.2.cloned.1.call-done), kind=kOutput, calls=%fused_computation.24 | convolution fusion | flops 1073741824 | bytes 6291456 | tf_op jit(solution)/shard_map/dot_general | solution.py:132
  65.7 0.0 copy-done.3
  65.7 0.0 copy-done.1
  65.8 0.0 copy-start.2
  65.8 0.0 copy-start.4
  65.8 0.8 fusion.6
  66.6 0.2 copy-done.2
  66.8 0.0 copy-done.4
  66.8 0.9 fusion.4
  67.7 16.9 %all_to_all.30 = bf16[4,128,1024]{2,1,0:T(8,128)(2,1)S(1)} all-to-all(bf16[4,128,1024]{2,1,0:T(8,128)(2,1)S(1)} %bitcast.38), channel_id=1, replica_groups=mesh['dp'=8,'ctx'=4] {'ctx'}, dimensions={0} | all-to-all | bytes 2097152 | tf_op jit(solution)/shard_map/all_to_all | solution.py:168
  84.6 1.6 %convert_bitcast_fusion = f32[128,4,1024]{2,0,1:T(8,128)} fusion(bf16[4,128,1024]{2,1,0:T(8,128)(2,1)S(1)} %all_to_all.30), kind=kLoop, calls=%fused_computation.14 | loop fusion | flops 524288 | bytes 3145728 | tf_op jit(solution)/shard_map/convert_element_type | solution.py:153
  86.1 1.9 %copy.23 = f32[128,4,1024]{0,2,1:T(8,128)S(1)} copy(f32[128,4,1024]{2,0,1:T(8,128)} %convert_bitcast_fusion) | data formatting | bytes 4194304 | tf_op jit(solution)/shard_map/convert_element_type | solution.py:153
  88.1 2.0 %fusion.5 = bf16[1,128,4096]{1,2,0:T(8,128)(2,1)S(1)} fusion(f32[128,4,1024]{0,2,1:T(8,128)S(1)} %copy.23, f32[128,3,4096]{0,2,1:T(8,128)} %copy-done), kind=kLoop, calls=%fused_computation.13 | loop fusion | flops 1572864 | bytes 4194304 | tf_op jit(solution)/shard_map/convert_element_type | solution.py:153
  90.1 1.3 %copy.24 = bf16[1,128,4096]{2,1,0:T(8,128)(2,1)} copy(bf16[1,128,4096]{1,2,0:T(8,128)(2,1)S(1)} %fusion.5) | data formatting | bytes 2097152 | tf_op jit(solution)/shard_map/convert_element_type | solution.py:153
  (1 shorter events, 0.0 us)
Async XLA Ops:
  6.5 56.2 %all-gather.2.cloned.1.call-start = ((), (), s32[]{:S(2)}) async-start(), calls=%async_computation.2 | async-start | bytes 1179648 | tf_op jit(solution)/shard_map/all_gather | solution.py:160
  7.5 13.0 %collective-permute-start = (bf16[2,3,4096]{2,0,1:T(2,128)(2,1)S(1)}, bf16[2,3,4096]{2,0,1:T(2,128)(2,1)S(1)}, u32[]{:S(2)}, u32[]{:S(2)}) collective-permute-start(bf16[2,3,4096]{2,0,1:T(2,128)(2,1)S(1)} %slice_bitcast_fusion.3), channel_id=1, source_target_pairs={{0,1},{1,2},{2,3},{4,5},{5,6},{6,7},{8,9},{9,10},{10,11},{12,13},{... | collective-permute-start | bytes 147464 | tf_op jit(solution)/shard_map/ppermute | solution.py:162
  36.9 2.7 %copy-start = (f32[128,3,4096]{0,2,1:T(8,128)}, f32[128,3,4096]{0,2,1:T(8,128)S(1)}, u32[]{:S(2)}) copy-start(f32[128,3,4096]{0,2,1:T(8,128)S(1)} %fusion) | copy-start | bytes 18874372
  62.8 3.0 %copy-start.3 = (bf16[512,512]{1,0:T(8,128)(2,1)S(1)}, bf16[512,512]{1,0:T(8,128)(2,1)}, u32[]{:S(2)}) copy-start(bf16[512,512]{1,0:T(8,128)(2,1)} %constant.10) | copy-start | bytes 1572868
  62.8 3.0 %copy-start.1 = (f32[1024,1024]{1,0:T(8,128)S(1)}, f32[1024,1024]{1,0:T(8,128)}, u32[]{:S(2)}) copy-start(f32[1024,1024]{1,0:T(8,128)} %fusion.8) | copy-start | bytes 12582916
  65.8 1.0 %copy-start.2 = (bf16[512,512]{1,0:T(8,128)(2,1)S(1)}, bf16[512,512]{1,0:T(8,128)(2,1)}, u32[]{:S(2)}) copy-start(bf16[512,512]{1,0:T(8,128)(2,1)} %constant.11) | copy-start | bytes 1572868
  65.8 1.0 %copy-start.4 = (f32[1024]{0:T(1024)S(1)}, f32[1024]{0:T(1024)}, u32[]{:S(2)}) copy-start(f32[1024]{0:T(1024)} %param.9) | copy-start | bytes 12292
Sparse Core Ops, SparseCore 0:
  10.0 42.7 all-gather.1
where the time goes:
time: 98.7 us; the launch traced here: 98.3 us
  blocking collectives  40.9 us (41%)
  other arithmetic  17.3 us (18%)
  local copies, waits for them, and re-layouts  15.1 us (15%)
  between operations  13.5 us (14%)
  matrix products  9.08 us (9%)
  starting transfers between devices  2.36 us (2%)
    all_to_all x1, blocking collectives, on_device(): lax.all_to_all(gated, 'ctx', split_axis=1, concat_axis=0, tiled=True)  16.9 us
    all_to_all x1, blocking collectives, on_device(): lax.all_to_all(response_slab, 'ctx', split_axis=0, concat_axis=1, tiled=T...  16.9 us
    add x1, other arithmetic, causal_short(): summed = summed + taps[tap_index] * widened[offset:offset + row_count]  9.39 us
    all_gather x1, blocking collectives, on_device(): all_taps = lax.all_gather(short_taps, 'ctx', axis=2, tiled=True)  7.11 us
    unnamed x11, local copies, waits for them, and re-layouts  6.44 us
    dot_general x1, matrix products, long_convolve(): sig = jnp.dot(forward, gated_slab, preferred_element_type=jnp.float32)  4.5 us
    convert_element_type x1, other arithmetic, causal_short(): widened = extended.astype(jnp.float32)  4.08 us
    dot_general x1, matrix products, long_convolve(): ker = jnp.dot(forward, filter_slab, preferred_element_type=jnp.float32)  2.94 us
  transfers between devices with their start and end apart: 2, of which 0 were waited for; matrix products, arithmetic and copies ran while one was open for 27% of the time, Pallas kernels for 0%

commit v1 on v0

--- a/solution.py
+++ b/solution.py
@@ -7,6 +7,33 @@
 
 RADIX = 64
 HIGH = lax.Precision.HIGHEST
+
+
+def entries_push(xs, ndim_at):
+    heard = list(xs.shape[1:])
+    heard[ndim_at] *= xs.shape[0]
+    passed = jnp.moveaxis(xs, 0, ndim_at).reshape(heard)
+    return passed
+
+
+def bands_lift(load, across):
+    o_now, w1 = (lax.axis_size(across), lax.axis_index(across))
+    out_arr, spare = (load[None], 1)
+    while spare < o_now:
+        built = lax.ppermute(
+            out_arr, axis_name=across, perm=list(map(lambda dd: (dd, dd ^ spare), range(o_now)))
+        )
+        current_block = w1 & spare == 0
+        out_arr = jnp.concatenate(
+            [jnp.where(current_block, out_arr, built), jnp.where(current_block, built, out_arr)]
+        )
+        spare *= 2
+    return out_arr
+
+
+def list_frame(inp, local_array, along_dim):
+    field_out = entries_push(bands_lift(inp, local_array), along_dim)
+    return field_out
 
 
 def causal_short(extended, taps, kernel_size):
@@ -158,7 +185,7 @@
     ctx_size = lax.axis_size("ctx")
     rows = projected[0]
     filter_slab = lax.all_gather(long_filter, "dp", axis=0, tiled=True)
-    all_taps = lax.all_gather(short_taps, "ctx", axis=2, tiled=True)
+    all_taps = list_frame(short_taps, "ctx", 2)
     halo = lax.ppermute(
         rows[-(kernel_size - 1) :], "ctx", [(i, i + 1) for i in range(ctx_size - 1)]
     )

time: 98.7 us -> 94.9 us (0.961)
  blocking collectives: 40.9 us -> 33.8 us
  starting transfers between devices: 2.36 us -> 5.42 us
    all_gather x1 -> x0, blocking collectives: 7.11 us -> none  [on_device(): all_taps = lax.all_gather(short_taps, 'ctx', axis=2, tiled=True)]
    ppermute x0 -> x2, starting transfers between devices: none -> 3.46 us  [bands_lift(): lax.ppermute(out_arr, axis_name=across, perm=list(map(lambda dd: (dd, dd...]
    unnamed x11 -> x13, local copies, waits for them, and re-layouts: 6.44 us -> 6.41 us
  transfers between devices with their start and end apart: 2 -> 4, of which waited for: 0 -> 0; matrix products, arithmetic and copies ran while one was open for 27% -> 29% of each run, Pallas kernels for 0% -> 0%
where the time goes in v1:
time: 94.9 us; the launch traced here: 94.5 us
  blocking collectives  33.8 us (36%)
  other arithmetic  17.5 us (18%)
  local copies, waits for them, and re-layouts  15.1 us (16%)
  between operations  13.6 us (14%)
  matrix products  9.1 us (10%)
  starting transfers between devices  5.42 us (6%)
    all_to_all x1, blocking collectives, on_device(): lax.all_to_all(gated, 'ctx', split_axis=1, concat_axis=0, tiled=True)  16.9 us
    all_to_all x1, blocking collectives, on_device(): lax.all_to_all(response_slab, 'ctx', split_axis=0, concat_axis=1, tiled=T...  16.9 us
    add x1, other arithmetic, causal_short(): summed = summed + taps[tap_index] * widened[offset:offset + row_count]  9.39 us
    unnamed x13, local copies, waits for them, and re-layouts  6.41 us
    dot_general x1, matrix products, long_convolve(): sig = jnp.dot(forward, gated_slab, preferred_element_type=jnp.float32)  4.52 us
    convert_element_type x1, other arithmetic, causal_short(): widened = extended.astype(jnp.float32)  4.15 us
    ppermute x2, starting transfers between devices, bands_lift(): lax.ppermute(out_arr, axis_name=across, perm=list(map(lambda dd: (dd, dd...  3.46 us
    dot_general x1, matrix products, long_convolve(): ker = jnp.dot(forward, filter_slab, preferred_element_type=jnp.float32)  2.94 us
  transfers between devices with their start and end apart: 4, of which 0 were waited for; matrix products, arithmetic and copies ran while one was open for 29% of the time, Pallas kernels for 0%

profile of v1, /device:TPU:0, one launch (start us, length us, event | category | flops | bytes accessed | tf_op | source)
XLA Modules:
  0.0 94.5 jit_solution(17045763314938171059)
XLA Ops:
  6.5 0.0 all-gather.2.cloned.1.call-start
  6.5 0.5 collective-permute-start
  7.0 1.0 %slice_bitcast_fusion = bf16[2,3,4096]{2,0,1:T(2,128)(2,1)S(1)} fusion(bf16[1,128,3,4096]{3,1,2,0:T(8,128)(2,1)} %param.6), kind=kLoop, calls=%fused_computation.21 | loop fusion | bytes 98304 | tf_op jit(solution)/shard_map/slice | solution.py:190
  8.0 2.0 %collective-permute-start.2 = (bf16[2,3,4096]{2,0,1:T(2,128)(2,1)S(1)}, bf16[2,3,4096]{2,0,1:T(2,128)(2,1)S(1)}, u32[]{:S(2)}, u32[]{:S(2)}) collective-permute-start(bf16[2,3,4096]{2,0,1:T(2,128)(2,1)S(1)} %slice_bitcast_fusion), channel_id=1, source_target_pairs={{0,1},{1,2},{2,3},{4,5},{5,6},{6,7},{8,9},{9,10},{10,11},{12,13},{... | collective-permute-start | bytes 147464 | tf_op jit(solution)/shard_map/ppermute | solution.py:189
  9.9 0.0 all-gather.2.cloned.1.call-update
  10.0 0.0 copy-start.4
  10.0 3.5 %copy.19 = bf16[1,128,3,4096]{1,3,2,0:T(8,128)(2,1)S(1)} copy(bf16[1,128,3,4096]{3,1,2,0:T(8,128)(2,1)} %param.6) | data formatting | bytes 6291456 | tf_op args[0]
  13.5 0.0 collective-permute-done
  13.5 0.0 copy-done.4
  13.6 3.0 %collective-permute-start.1 = (f32[2,3,3,1024]{3,2,1,0:T(4,128)S(1)}, f32[2,3,3,1024]{3,2,1,0:T(4,128)S(1)}, u32[]{:S(2)}, u32[]{:S(2)}) collective-permute-start(f32[2,3,3,1024]{3,2,1,0:T(4,128)S(1)} %pad_maximum_fusion), channel_id=1, source_target_pairs={{0,2},{1,3},{2,0},{3,1},{4,6},{5,7},{6,4},{7,5},{8,10},{9,11},{10,... | collective-permute-start | bytes 221192 | tf_op jit(solution)/shard_map/ppermute | solution.py:23
  16.6 0.0 collective-permute-done.2
  16.6 2.8 %copy.20 = bf16[2,3,4096]{0,2,1:T(8,128)(2,1)} copy(bf16[2,3,4096]{2,0,1:T(2,128)(2,1)S(1)} %collective-permute-done.2) | data formatting | bytes 98304 | tf_op jit(solution)/shard_map/ppermute | solution.py:189
  19.4 4.1 %maximum_convert_fusion = f32[130,3,4096]{0,2,1:T(8,128)S(1)} fusion(bf16[128,3,4096]{0,2,1:T(8,128)(2,1)S(1)} %bitcast.38, bf16[2,3,4096]{0,2,1:T(8,128)(2,1)} %copy.20), kind=kLoop, calls=%fused_computation.5 | loop fusion | flops 6389760 | bytes 9584640 | tf_op jit(solution)/shard_map/convert_element_type | solution.py:41
  23.5 0.0 collective-permute-done.1
  23.7 9.4 %fusion = f32[128,3,4096]{0,2,1:T(8,128)S(1)} fusion(f32[130,3,4096]{0,2,1:T(8,128)S(1)} %maximum_convert_fusion, f32[3,4096]{1,0:T(4,128)S(1)} %bitcast.42, f32[3,4096]{1,0:T(4,128)S(1)} %bitcast.43, f32[3,4096]{1,0:T(4,128)S(1)} %bitcast.41), kind=kLoop, calls=%fused_computation.1 | loop fusion | flops 7864320 | bytes 25313280 | tf_op jit(solution)/shard_map/add | solution.py:45
  33.1 0.0 copy-start
  33.1 2.6 %copy-done = f32[128,3,4096]{0,2,1:T(8,128)} copy-done((f32[128,3,4096]{0,2,1:T(8,128)}, f32[128,3,4096]{0,2,1:T(8,128)S(1)}, u32[]{:S(2)}) %copy-start) | copy-done | bytes 6291480
  35.7 0.2 fusion.2
  35.9 0.5 copy.21
  36.5 16.9 %all_to_all.29 = bf16[128,4,1024]{2,0,1:T(8,128)(2,1)S(1)} all-to-all(bf16[128,4,1024]{2,0,1:T(8,128)(2,1)S(1)} %copy.21), channel_id=1, replica_groups=mesh['dp'=8,'ctx'=4] {'ctx'}, dimensions={1} | all-to-all | bytes 2097152 | tf_op jit(solution)/shard_map/all_to_all | solution.py:193
  53.4 0.8 copy.22
  54.2 0.3 reshape.53
  54.5 4.5 %fusion.9 = f32[1024,1024]{1,0:T(8,128)} fusion(bf16[1024,512]{1,0:T(8,128)(2,1)} %constant.19, bf16[512,1024]{1,0:T(8,128)(2,1)S(1)} %reshape.53), kind=kOutput, calls=%fused_computation.27 | convolution fusion | flops 1073741824 | bytes 6291456 | tf_op jit(solution)/shard_map/dot_general | solution.py:158
  59.0 0.0 copy-start.3
  59.0 0.0 all-gather.2.cloned.1.call-done
  59.0 0.0 copy-start.1
  59.0 2.9 %fusion.10 = f32[1024,1024]{1,0:T(8,128)S(1)} fusion(bf16[1024,512]{1,0:T(8,128)(2,1)} %constant.14.clone, bf16[512,1024]{1,0:T(8,128)(2,1)} %all-gather.2.cloned.1.call-done), kind=kOutput, calls=%fused_computation.28 | convolution fusion | flops 1073741824 | bytes 6291456 | tf_op jit(solution)/shard_map/dot_general | solution.py:159
  61.9 0.0 copy-done.3
  61.9 0.0 copy-done.1
  62.0 0.0 copy-start.2
  62.0 0.0 copy-start.5
  62.0 0.8 fusion.6
  62.8 0.2 copy-done.2
  63.0 0.0 copy-done.5
  63.0 0.9 fusion.4
  63.9 16.9 %all_to_all.30 = bf16[4,128,1024]{2,1,0:T(8,128)(2,1)S(1)} all-to-all(bf16[4,128,1024]{2,1,0:T(8,128)(2,1)S(1)} %bitcast.40), channel_id=1, replica_groups=mesh['dp'=8,'ctx'=4] {'ctx'}, dimensions={0} | all-to-all | bytes 2097152 | tf_op jit(solution)/shard_map/all_to_all | solution.py:195
  80.8 1.6 %convert_bitcast_fusion = f32[128,4,1024]{2,0,1:T(8,128)} fusion(bf16[4,128,1024]{2,1,0:T(8,128)(2,1)S(1)} %all_to_all.30), kind=kLoop, calls=%fused_computation.14 | loop fusion | flops 524288 | bytes 3145728 | tf_op jit(solution)/shard_map/convert_element_type | solution.py:180
  82.4 1.9 %copy.23 = f32[128,4,1024]{0,2,1:T(8,128)S(1)} copy(f32[128,4,1024]{2,0,1:T(8,128)} %convert_bitcast_fusion) | data formatting | bytes 4194304 | tf_op jit(solution)/shard_map/convert_element_type | solution.py:180
  84.3 2.0 %fusion.5 = bf16[1,128,4096]{1,2,0:T(8,128)(2,1)S(1)} fusion(f32[128,4,1024]{0,2,1:T(8,128)S(1)} %copy.23, f32[128,3,4096]{0,2,1:T(8,128)} %copy-done), kind=kLoop, calls=%fused_computation.13 | loop fusion | flops 1572864 | bytes 4194304 | tf_op jit(solution)/shard_map/convert_element_type | solution.py:180
  86.3 1.3 %copy.24 = bf16[1,128,4096]{2,1,0:T(8,128)(2,1)} copy(bf16[1,128,4096]{1,2,0:T(8,128)(2,1)S(1)} %fusion.5) | data formatting | bytes 2097152 | tf_op jit(solution)/shard_map/convert_element_type | solution.py:180
  (5 shorter events, 0.2 us)
Async XLA Ops:
  6.5 52.5 %all-gather.2.cloned.1.call-start = ((), (), s32[]{:S(2)}) async-start(), calls=%async_computation.2 | async-start | bytes 1179648 | tf_op jit(solution)/shard_map/all_gather | solution.py:187
  6.5 7.0 %collective-permute-start = (f32[1,3,3,1024]{3,2,1,0:T(4,128)}, f32[1,3,3,1024]{3,2,1,0:T(4,128)S(1)}, u32[]{:S(2)}, u32[]{:S(2)}) collective-permute-start(f32[1,3,3,1024]{3,2,1,0:T(4,128)} %bitcast.44), channel_id=1, source_target_pairs={{0,1},{1,0},{2,3},{3,2},{4,5},{5,4},{6,7},{7,6},{8,9},{9,8},{10,11... | collective-permute-start | bytes 110600 | tf_op jit(solution)/shard_map/ppermute | solution.py:23
  8.0 8.6 %collective-permute-start.2 = (bf16[2,3,4096]{2,0,1:T(2,128)(2,1)S(1)}, bf16[2,3,4096]{2,0,1:T(2,128)(2,1)S(1)}, u32[]{:S(2)}, u32[]{:S(2)}) collective-permute-start(bf16[2,3,4096]{2,0,1:T(2,128)(2,1)S(1)} %slice_bitcast_fusion), channel_id=1, source_target_pairs={{0,1},{1,2},{2,3},{4,5},{5,6},{6,7},{8,9},{9,10},{10,11},{12,13},{... | collective-permute-start | bytes 147464 | tf_op jit(solution)/shard_map/ppermute | solution.py:189
  10.0 3.5 %copy-start.4 = (f32[3,3,1024]{2,1,0:T(4,128)S(1)}, f32[3,3,1024]{2,1,0:T(4,128)}, u32[]{:S(2)}) copy-start(f32[3,3,1024]{2,1,0:T(4,128)} %param.7) | copy-start | bytes 110596
  13.6 10.0 %collective-permute-start.1 = (f32[2,3,3,1024]{3,2,1,0:T(4,128)S(1)}, f32[2,3,3,1024]{3,2,1,0:T(4,128)S(1)}, u32[]{:S(2)}, u32[]{:S(2)}) collective-permute-start(f32[2,3,3,1024]{3,2,1,0:T(4,128)S(1)} %pad_maximum_fusion), channel_id=1, source_target_pairs={{0,2},{1,3},{2,0},{3,1},{4,6},{5,7},{6,4},{7,5},{8,10},{9,11},{10,... | collective-permute-start | bytes 221192 | tf_op jit(solution)/shard_map/ppermute | solution.py:23
  33.1 2.6 %copy-start = (f32[128,3,4096]{0,2,1:T(8,128)}, f32[128,3,4096]{0,2,1:T(8,128)S(1)}, u32[]{:S(2)}) copy-start(f32[128,3,4096]{0,2,1:T(8,128)S(1)} %fusion) | copy-start | bytes 18874372
  59.0 3.0 %copy-start.3 = (bf16[512,512]{1,0:T(8,128)(2,1)S(1)}, bf16[512,512]{1,0:T(8,128)(2,1)}, u32[]{:S(2)}) copy-start(bf16[512,512]{1,0:T(8,128)(2,1)} %constant.20) | copy-start | bytes 1572868
  59.0 3.0 %copy-start.1 = (f32[1024,1024]{1,0:T(8,128)S(1)}, f32[1024,1024]{1,0:T(8,128)}, u32[]{:S(2)}) copy-start(f32[1024,1024]{1,0:T(8,128)} %fusion.9) | copy-start | bytes 12582916
  62.0 1.0 %copy-start.2 = (bf16[512,512]{1,0:T(8,128)(2,1)S(1)}, bf16[512,512]{1,0:T(8,128)(2,1)}, u32[]{:S(2)}) copy-start(bf16[512,512]{1,0:T(8,128)(2,1)} %constant.21) | copy-start | bytes 1572868
  62.0 1.0 %copy-start.5 = (f32[1024]{0:T(1024)S(1)}, f32[1024]{0:T(1024)}, u32[]{:S(2)}) copy-start(f32[1024]{0:T(1024)} %param.9) | copy-start | bytes 12292
Sparse Core Ops, SparseCore 0:
  10.1 42.8 all-gather.1
